TPU v7x, 32 devices: a whole 2x2x4 slice. The times are simulated.
32 devices in a mesh: groups: 2 (over y), seq: 8 (over z, x), head: 2 (over core).
Axes of the slice: x: 2, y: 2, z: 4, core: 2. Of those that a mesh axis runs over, the one named last changes fastest.
Arguments:
- queries: bfloat16 [2048, 1024], P(('groups', 'seq'), 'head'), parts along dimension 0, may hold values from -600 to 600
- keys: bfloat16 [2048, 1024], P(('groups', 'seq'), 'head'), parts along dimension 0, may hold values from -600 to 600
- values: bfloat16 [2048, 1024], P(('groups', 'seq'), 'head'), parts along dimension 0, may hold values from -600 to 600
- out_weight: bfloat16 [2048, 1024], P('seq', 'head'), may hold values from -0.1875 to 0.1875
- grad_y: bfloat16 [2048, 2048], P(('groups', 'seq')), parts along dimension 0, may hold values from -6 to 6
Outputs:
- out_y: bfloat16 [2048, 2048], P(('groups', 'seq')), parts along dimension 0
- grad_queries: bfloat16 [2048, 1024], P(('groups', 'seq'), 'head'), parts along dimension 0
- grad_keys: bfloat16 [2048, 1024], P(('groups', 'seq'), 'head'), parts along dimension 0
- grad_values: bfloat16 [2048, 1024], P(('groups', 'seq'), 'head'), parts along dimension 0
- grad_weight: float32 [4096, 1024], P(('groups', 'seq'), 'head'), parts along dimension 0
There are 2 independent parts, one for each index of `groups`. A program takes and returns all parts, laid end to end along the dimension named above; an argument that names none is the same for every part. Nothing has to cross between parts.
All inputs are finite; a program needn't handle non-finite values.
Results may differ from a plain program's by a relative error of at most 0.009.
Values may be sent and summed in bfloat16 or wider, within the bound.
No kernel may reach another device: no remote copies, remote signals or barrier semaphores. Data moves between devices by JAX's collectives and lax.ppermute only.
A program may use at most 192 MiB of HBM per device.

v0:
```python
import jax
import jax.numpy as jnp
from jax import lax
from jax.sharding import PartitionSpec as P

DH = 128
TILE = 128
epsilon = 1e-06


def carried_in(value, axis, join, neutral, backward):
    count, mine = (lax.axis_size(axis), lax.axis_index(axis))
    pieces = lax.all_gather(value, axis)
    if backward:
        pieces = pieces[::-1]
        mine = count - 1 - mine
    so_far = jnp.full_like(value, 0) + jnp.asarray(neutral, value.dtype)

    def turn(position, so_far):
        longer = join(so_far, pieces[position])
        return jnp.where(position < mine, longer, so_far)

    return lax.fori_loop(0, count - 1, turn, so_far)


def add_states(earlier, later):
    return earlier + later


def on_device(queries, keys, values, out_weight, grad_y):
    row_count = queries.shape[0]
    tile_count = row_count // TILE
    head_count = queries.shape[1] // DH

    def tiled(array):
        return array.reshape(tile_count, TILE, head_count, DH)

    query_tiles = tiled(queries)
    key_tiles = tiled(keys)
    value_tiles = tiled(values)
    causal = lax.broadcasted_iota(jnp.int32, (TILE, TILE), 0) >= lax.broadcasted_iota(
        jnp.int32, (TILE, TILE), 1
    )
    raw_scores = jnp.einsum(
        "nthd,nshd->nhts", query_tiles, key_tiles, preferred_element_type=jnp.float32
    )
    scores = jnp.where(causal, raw_scores, 0.0).astype(jnp.bfloat16)
    states = jnp.einsum(
        "nshd,nshe->nhde", key_tiles, value_tiles, preferred_element_type=jnp.float32
    )
    empty_state = jnp.zeros(states.shape[1:], jnp.float32)
    device_prefix = carried_in(jnp.sum(states, axis=0), "seq", add_states, empty_state, False)
    prefix_state = (device_prefix[None] + (jnp.cumsum(states, axis=0) - states)).astype(
        jnp.bfloat16
    )
    attended = jnp.einsum(
        "nhts,nshe->nthe", scores, value_tiles, preferred_element_type=jnp.float32
    )
    attended = attended + jnp.einsum(
        "nthd,nhde->nthe", query_tiles, prefix_state, preferred_element_type=jnp.float32
    )
    inverse_rms = lax.rsqrt(jnp.mean(attended * attended, axis=-1, keepdims=True) + epsilon)
    normed_exact = attended * inverse_rms
    normed = normed_exact.astype(jnp.bfloat16).reshape(row_count, -1)
    contract_last = (((1,), (1,)), ((), ()))
    back_weight = lax.all_gather(out_weight, "seq", axis=0, tiled=True)
    grad_normed = jnp.dot(grad_y, back_weight, preferred_element_type=jnp.float32)
    fore_weight = lax.all_gather(out_weight, "seq", axis=0, tiled=True)
    partial_out = lax.dot_general(
        normed, fore_weight, contract_last, preferred_element_type=jnp.float32
    )
    out_y = lax.psum(partial_out.astype(jnp.bfloat16), "head")
    grad_tiles = tiled(grad_normed)
    projected = jnp.mean(grad_tiles * normed_exact, axis=-1, keepdims=True)
    grad_out = (inverse_rms * (grad_tiles - normed_exact * projected)).astype(jnp.bfloat16)
    raw_grad = jnp.einsum(
        "nthe,nshe->nhts", grad_out, value_tiles, preferred_element_type=jnp.float32
    )
    grad_scores = jnp.where(causal, raw_grad, 0.0).astype(jnp.bfloat16)
    adjoint = jnp.einsum(
        "nthd,nthe->nhde", query_tiles, grad_out, preferred_element_type=jnp.float32
    )
    own_adjoint = jnp.sum(adjoint, axis=0)
    device_suffix = carried_in(own_adjoint, "seq", add_states, empty_state, True)
    later_tiles = jnp.flip(jnp.cumsum(jnp.flip(adjoint, 0), axis=0), 0) - adjoint
    suffix_state = (device_suffix[None] + later_tiles).astype(jnp.bfloat16)
    grad_queries = jnp.einsum(
        "nhts,nshd->nthd", grad_scores, key_tiles, preferred_element_type=jnp.float32
    )
    grad_queries = grad_queries + jnp.einsum(
        "nthe,nhde->nthd", grad_out, prefix_state, preferred_element_type=jnp.float32
    )
    grad_keys = jnp.einsum(
        "nhts,nthd->nshd", grad_scores, query_tiles, preferred_element_type=jnp.float32
    )
    grad_keys = grad_keys + jnp.einsum(
        "nshe,nhde->nshd", value_tiles, suffix_state, preferred_element_type=jnp.float32
    )
    grad_values = jnp.einsum(
        "nhts,nthe->nshe", scores, grad_out, preferred_element_type=jnp.float32
    )
    grad_values = grad_values + jnp.einsum(
        "nshd,nhde->nshe", key_tiles, suffix_state, preferred_element_type=jnp.float32
    )
    grad_weight = lax.psum_scatter(
        lax.dot_general(
            grad_y, normed, (((0,), (0,)), ((), ())), preferred_element_type=jnp.float32
        ),
        "seq",
        scatter_dimension=0,
        tiled=True,
    )
    return (
        out_y,
        grad_queries.reshape(row_count, -1).astype(jnp.bfloat16),
        grad_keys.reshape(row_count, -1).astype(jnp.bfloat16),
        grad_values.reshape(row_count, -1).astype(jnp.bfloat16),
        grad_weight,
    )


def solution(mesh):
    placed = (
        P(("groups", "seq"), "head"),
        P(("groups", "seq"), "head"),
        P(("groups", "seq"), "head"),
        P("seq", "head"),
        P(("groups", "seq"), None),
    )
    return jax.shard_map(
        on_device,
        mesh=mesh,
        in_specs=placed,
        out_specs=(
            P(("groups", "seq"), None),
            P(("groups", "seq"), "head"),
            P(("groups", "seq"), "head"),
            P(("groups", "seq"), "head"),
            P(("groups", "seq"), "head"),
        ),
        check_vma=False,
    )
```

profile of v0, /device:TPU:0, one launch (start us, length us, event | category | flops | bytes accessed | tf_op | source)
XLA Modules:
  0.0 284.6 jit_solution(14528810327368836696)
XLA Ops:
  7.2 0.0 copy-start
  7.2 0.0 all-gather.8.cloned.1.call-start
  7.2 1.1 copy.104
  8.3 0.0 copy-start.4
  8.3 1.8 fusion.10
  10.1 0.0 all-gather.8.cloned.1.call-update
  10.2 0.0 all-gather.6.cloned.1.call-start
  10.2 0.7 all-gather.6.cloned.1.call-update
  10.9 0.0 all-gather.10.cloned.1.call-start
  11.0 1.2 fusion.1
  12.2 0.6 copy-done.9
  12.8 1.1 convolution_bitcast_fusion.4
  14.0 0.0 copy-start.2
  14.0 48.7 %all-gather.8.cloned.1.call-done = f32[32,128,128]{2,1,0:T(8,128)} async-done(((f32[4,128,128]{2,1,0:T(8,128)}), f32[32,128,128]{2,1,0:T(8,128)}) %all-gather.8.cloned.1.call-update) | async-done | bytes 2097168 | tf_op jit(solution)/shard_map/all_gather | solution.py:13
  62.7 7.5 %while.28 = (s32[]{:T(128)}, f32[4,128,128]{2,1,0:T(8,128)S(1)}, s32[]{:T(128)}, f32[8,4,128,128]{3,2,1,0:T(8,128)}, s32[]{:T(128)}, /*index=5*/s32[]{:T(128)}) while((s32[]{:T(128)}, f32[4,128,128]{2,1,0:T(8,128)S(1)}, s32[]{:T(128)}, f32[8,4,128,128]{3,2,1,0:T(8,128)}, s32[]{:T(128)}, /*index=5*/s32[]{:T(128)}) %tuple.84), condition=%wide.region_1.2_spmd.clone, body=%wide.region_0.1_spmd.clone.sunk | while | flops 196612 | bytes 786533 | solution.py:23
  62.7 1.1 add_select_fusion.4
  63.8 1.0 add_select_fusion.4
  64.9 1.0 add_select_fusion.4
  66.0 1.0 add_select_fusion.4
  67.0 1.0 add_select_fusion.4
  68.1 1.0 add_select_fusion.4
  69.2 1.0 add_select_fusion.4
  70.3 0.3 multiply_reduce_fusion.1
  70.5 42.1 %all-gather.6.cloned.1.call-done = bf16[2048,512]{1,0:T(8,128)(2,1)} async-done(((bf16[256,512]{1,0:T(8,128)(2,1)}), bf16[2048,512]{1,0:T(8,128)(2,1)}) %all-gather.6.cloned.1.call-update) | async-done | bytes 2097168 | tf_op jit(solution)/shard_map/all_gather | solution.py:68
  112.7 2.5 fusion.28
  115.2 0.1 fusion.6
  115.3 0.0 copy-start.6
  115.3 0.2 convolution_bitcast_fusion.2
  115.5 0.8 copy.47
  116.3 0.0 all-gather.10.cloned.1.call-update
  116.4 0.0 reduce-scatter.2.cloned.1.call-start
  116.4 2.7 convolution_bitcast_fusion
  119.1 0.0 reduce-scatter.2.cloned.1.call-update
  119.1 0.0 all-reduce.2.cloned.1.call-start
  119.2 0.8 copy-done.3
  120.0 0.2 fusion.2
  120.2 0.0 copy-start.10
  120.2 1.2 convolution_bitcast_fusion.3
  121.4 0.8 fusion.3
  122.2 1.7 copy.52
  123.9 1.9 convolution_bitcast_fusion.1
  125.8 1.8 fusion.29
  127.6 2.5 convolution_convert_fusion
  130.1 0.0 all-reduce.2.cloned.1.call-update
  130.2 34.2 %all-gather.10.cloned.1.call-done = f32[32,128,128]{2,1,0:T(8,128)} async-done(((f32[4,128,128]{2,1,0:T(8,128)}), f32[32,128,128]{2,1,0:T(8,128)}) %all-gather.10.cloned.1.call-update) | async-done | bytes 2097168 | tf_op jit(solution)/shard_map/all_gather | solution.py:13
  164.3 1.7 rev.3
  166.1 0.8 while.29
  166.1 0.1 add_select_fusion.5
  166.2 0.1 add_select_fusion.5
  166.3 0.1 add_select_fusion.5
  166.4 0.1 add_select_fusion.5
  166.5 0.1 add_select_fusion.5
  166.7 0.1 add_select_fusion.5
  166.8 0.1 add_select_fusion.5
  166.9 0.0 copy-start.8
  166.9 0.1 copy.48
  167.1 1.2 fusion.4
  168.2 0.8 copy.53
  169.0 0.2 fusion.5
  169.2 0.8 copy.54
  170.0 84.8 %reduce-scatter.2.cloned.1.call-done = f32[256,512]{0,1:T(8,128)} async-done(((f32[2048,512]{0,1:T(8,128)}), f32[256,512]{0,1:T(8,128)}) %reduce-scatter.2.cloned.1.call-update) | async-done | bytes 524304 | tf_op jit(solution)/shard_map/reduce_scatter | solution.py:105
  254.8 2.0 copy.55
  256.8 19.4 %all-reduce.2.cloned.1.call-done = bf16[128,2048]{1,0:T(8,128)(2,1)} async-done(((bf16[128,2048]{1,0:T(8,128)(2,1)}), bf16[128,2048]{1,0:T(8,128)(2,1)}) %all-reduce.2.cloned.1.call-update) | async-done | bytes 524304 | tf_op jit(solution)/shard_map/psum | solution.py:72
  276.2 1.9 copy.120
  (22 shorter events, 0.2 us)
Async XLA Ops:
  7.2 105.5 %copy-start = (bf16[128,2048]{1,0:T(8,128)(2,1)S(1)}, bf16[128,2048]{1,0:T(8,128)(2,1)}, u32[]{:S(2)}) copy-start(bf16[128,2048]{1,0:T(8,128)(2,1)} %param.13) | copy-start | bytes 1572868
  7.2 55.6 %all-gather.8.cloned.1.call-start = ((), (), s32[]{:S(2)}) async-start(), calls=%async_computation.4 | async-start | bytes 2359296 | tf_op jit(solution)/shard_map/all_gather | solution.py:13
  8.3 2.6 copy-start.4
  10.2 102.5 %all-gather.6.cloned.1.call-start = ((), (), s32[]{:S(2)}) async-start(), calls=%async_computation.1 | async-start | bytes 2359296 | tf_op jit(solution)/shard_map/all_gather | solution.py:68
  10.9 153.4 %all-gather.10.cloned.1.call-start = ((), (), s32[]{:S(2)}) async-start(), calls=%async_computation.5 | async-start | bytes 2359296 | tf_op jit(solution)/shard_map/all_gather | solution.py:13
  12.2 0.6 copy-start.9
  14.0 56.2 %copy-start.2 = (f32[4,128,128]{2,1,0:T(8,128)S(1)}, f32[4,128,128]{2,1,0:T(8,128)}, u32[]{:S(2)}) copy-start(f32[4,128,128]{2,1,0:T(8,128)} %fusion.10) | copy-start | bytes 786436
  62.7 7.5 %copy-start.5 = (bf16[128,512]{1,0:T(8,128)(2,1)S(1)}, bf16[128,512]{1,0:T(8,128)(2,1)}, u32[]{:S(2)}) copy-start(bf16[128,512]{1,0:T(8,128)(2,1)} %param.9) | copy-start | bytes 393220
  115.3 3.7 %copy-start.6 = (bf16[1,128,4,128]{1,3,2,0:T(8,128)(2,1)}, bf16[1,128,4,128]{1,3,2,0:T(8,128)(2,1)S(1)}, u32[]{:S(2)}) copy-start(bf16[1,128,4,128]{1,3,2,0:T(8,128)(2,1)S(1)} %get-tuple-element.222) | copy-start | bytes 393220
  116.4 138.5 %reduce-scatter.2.cloned.1.call-start = ((), (), s32[]{:S(2)}) async-start(), calls=%async_computation.3 | async-start | bytes 4718592 | tf_op jit(solution)/shard_map/reduce_scatter | solution.py:105
  119.1 0.9 copy-start.3
  119.1 8.5 %copy-start.1 = (bf16[2048,512]{1,0:T(8,128)(2,1)S(1)}, bf16[2048,512]{1,0:T(8,128)(2,1)}, u32[]{:S(2)}) copy-start(bf16[2048,512]{1,0:T(8,128)(2,1)} %all-gather.6.cloned.1.call-done) | copy-start | bytes 6291460
  119.1 157.1 %all-reduce.2.cloned.1.call-start = ((), (), s32[]{:S(2)}) async-start(), calls=%async_computation.2 | async-start | bytes 1048576 | tf_op jit(solution)/shard_map/psum | solution.py:72
  120.2 2.0 copy-start.10
  166.1 2.9 %copy-start.7 = (f32[4,128,128]{2,1,0:T(8,128)S(1)}, f32[4,128,128]{2,1,0:T(8,128)}, u32[]{:S(2)}) copy-start(f32[4,128,128]{2,1,0:T(8,128)} %fusion.29) | copy-start | bytes 786436
  166.9 2.2 copy-start.8
Sparse Core Ops, SparseCore 0:
  10.7 51.9 all-gather.7
  64.9 47.7 all-gather.5
  116.5 47.8 all-gather.9
  167.8 86.9 reduce-scatter.1
  257.7 18.4 all-reduce.1
where the time goes:
time: 285 us
  waiting for transfers between devices  230 us (81%)
  matrix products  19.6 us (7%)
  between operations  14 us (5%)
  local copies, waits for them, and re-layouts  12.4 us (4%)
  other arithmetic  8.1 us (3%)
    reduce_scatter x1, waiting for transfers between devices, on_device(): lax.psum_scatter(lax.dot_general(grad_y, normed, (((0,), (0,)), ((), ()))...  84.8 us
    all_gather x2, waiting for transfers between devices, carried_in(): pieces = lax.all_gather(value, axis)  82.9 us
    all_gather x1, waiting for transfers between devices, on_device(): fore_weight = lax.all_gather(out_weight, 'seq', axis=0, tiled=True)  42.1 us
    psum x1, waiting for transfers between devices, on_device(): out_y = lax.psum(partial_out.astype(jnp.bfloat16), 'head')  19.4 us
    unnamed x27, local copies, waits for them, and re-layouts  8.63 us
    select_n x14, other arithmetic, turn(): return jnp.where(position < mine, longer, so_far)  7.89 us
  transfers between devices with their start and end apart: 5, of which 5 were waited for; matrix products, arithmetic and copies ran while one was open for 11% of the time, Pallas kernels for 0%

commit v1 on v0

--- a/solution.py
+++ b/solution.py
@@ -65,7 +65,26 @@
     contract_last = (((1,), (1,)), ((), ()))
     back_weight = lax.all_gather(out_weight, "seq", axis=0, tiled=True)
     grad_normed = jnp.dot(grad_y, back_weight, preferred_element_type=jnp.float32)
-    fore_weight = lax.all_gather(out_weight, "seq", axis=0, tiled=True)
+    peers, index, rows = (lax.axis_size("seq"), lax.axis_index("seq"), out_weight.shape[0])
+    forward = [(i, (i + 1) % peers) for i in range(peers)]
+    left = [(i, (i - 1) % peers) for i in range(peers)]
+    out = jnp.zeros(
+        (*out_weight.shape[:0], peers * rows, *out_weight.shape[0 + 1 :]), out_weight.dtype
+    )
+    out = lax.dynamic_update_slice_in_dim(out, out_weight, index * rows, axis=0)
+    from_left = from_right = out_weight
+    half = peers // 2
+    for turn_2 in range(1, half + 1):
+        from_left = lax.ppermute(from_left, "seq", forward)
+        out = lax.dynamic_update_slice_in_dim(
+            out, from_left, (index - turn_2) % peers * rows, axis=0
+        )
+        if turn_2 < peers - half:
+            from_right = lax.ppermute(from_right, "seq", left)
+            out = lax.dynamic_update_slice_in_dim(
+                out, from_right, (index + turn_2) % peers * rows, axis=0
+            )
+    fore_weight = out
     partial_out = lax.dot_general(
         normed, fore_weight, contract_last, preferred_element_type=jnp.float32
     )

time: 285 us -> 308 us (1.081)
  starting transfers between devices: 0.2 us -> 15.4 us
  waiting for transfers between devices: 230 us -> 235 us
  local copies, waits for them, and re-layouts: 12.4 us -> 15.9 us
    ppermute x0 -> x7, waiting for transfers between devices: none -> 39.7 us  [the longest x4 37.8 us: on_device(): from_left = lax.ppermute(from_left, 'seq', forward)]
    all_gather x2, waiting for transfers between devices: 82.9 us -> 49.3 us  [carried_in(): pieces = lax.all_gather(value, axis)]
    ppermute x0 -> x7, starting transfers between devices: none -> 15.2 us  [the longest x4 8 us: on_device(): from_left = lax.ppermute(from_left, 'seq', forward)]
    dynamic_update_slice x0 -> x8, local copies, waits for them, and re-layouts: none -> 3.97 us  [the longest x4 1.98 us: on_device(): lax.dynamic_update_slice_in_dim(out, from_left, (index - turn_2) % peers...]
    unnamed x27 -> x29, local copies, waits for them, and re-layouts: 8.63 us -> 8.06 us
  transfers between devices with their start and end apart: 5 -> 12, of which waited for: 5 -> 9; matrix products, arithmetic and copies ran while one was open for 11% -> 11% of each run, Pallas kernels for 0% -> 0%
where the time goes in v1:
time: 308 us; the launch traced here: 307 us
  waiting for transfers between devices  235 us (76%)
  matrix products  18.6 us (6%)
  local copies, waits for them, and re-layouts  15.9 us (5%)
  starting transfers between devices  15.4 us (5%)
  between operations  14.3 us (5%)
  other arithmetic  8.11 us (3%)
    reduce_scatter x1, waiting for transfers between devices, on_device(): lax.psum_scatter(lax.dot_general(grad_y, normed, (((0,), (0,)), ((), ()))...  83.4 us
    all_gather x2, waiting for transfers between devices, carried_in(): pieces = lax.all_gather(value, axis)  49.3 us
    all_gather x1, waiting for transfers between devices, on_device(): back_weight = lax.all_gather(out_weight, 'seq', axis=0, tiled=True)  42.1 us
    ppermute x4, waiting for transfers between devices, on_device(): from_left = lax.ppermute(from_left, 'seq', forward)  37.8 us
    psum x1, waiting for transfers between devices, on_device(): out_y = lax.psum(partial_out.astype(jnp.bfloat16), 'head')  19.4 us
    unnamed x29, local copies, waits for them, and re-layouts  8.06 us
    ppermute x4, starting transfers between devices, on_device(): from_left = lax.ppermute(from_left, 'seq', forward)  8 us
    select_n x14, other arithmetic, turn(): return jnp.where(position < mine, longer, so_far)  7.89 us
  transfers between devices with their start and end apart: 12, of which 9 were waited for; matrix products, arithmetic and copies ran while one was open for 11% of the time, Pallas kernels for 0%

profile of v1, /device:TPU:0, one launch (start us, length us, event | category | flops | bytes accessed | tf_op | source)
XLA Modules:
  0.0 307.4 jit_solution(10749797592657395628)
XLA Ops:
  7.2 1.1 copy.104
  8.3 1.8 fusion.10
  10.2 0.7 all-gather.6.cloned.1.call-update
  11.0 1.2 fusion.1
  12.2 1.2 convolution_bitcast_fusion.4
  13.4 49.3 %all-gather.8.cloned.1.call-done = f32[32,128,128]{2,1,0:T(8,128)} async-done(((f32[4,128,128]{2,1,0:T(8,128)}), f32[32,128,128]{2,1,0:T(8,128)}) %all-gather.8.cloned.1.call-update) | async-done | bytes 2097168 | tf_op jit(solution)/shard_map/all_gather | solution.py:13
  62.7 7.5 %while.28 = (s32[]{:T(128)}, f32[4,128,128]{2,1,0:T(8,128)S(1)}, s32[]{:T(128)}, f32[8,4,128,128]{3,2,1,0:T(8,128)}, s32[]{:T(128)}, /*index=5*/s32[]{:T(128)}) while((s32[]{:T(128)}, f32[4,128,128]{2,1,0:T(8,128)S(1)}, s32[]{:T(128)}, f32[8,4,128,128]{3,2,1,0:T(8,128)}, s32[]{:T(128)}, /*index=5*/s32[]{:T(128)}) %tuple.84), condition=%wide.region_1.2_spmd.clone, body=%wide.region_0.1_spmd.clone.sunk | while | flops 196612 | bytes 786525 | solution.py:23
  62.7 1.1 add_select_fusion.4
  63.8 1.0 add_select_fusion.4
  64.9 1.0 add_select_fusion.4
  66.0 1.0 add_select_fusion.4
  67.0 1.0 add_select_fusion.4
  68.1 1.0 add_select_fusion.4
  69.2 1.0 add_select_fusion.4
  70.3 0.3 multiply_reduce_fusion.1
  70.5 42.1 %all-gather.6.cloned.1.call-done = bf16[2048,512]{1,0:T(8,128)(2,1)} async-done(((bf16[256,512]{1,0:T(8,128)(2,1)}), bf16[2048,512]{1,0:T(8,128)(2,1)}) %all-gather.6.cloned.1.call-update) | async-done | bytes 2097168 | tf_op jit(solution)/shard_map/all_gather | solution.py:66
  112.7 2.5 fusion.28
  115.3 0.1 fusion.6
  115.3 0.2 convolution_bitcast_fusion.2
  115.5 0.8 copy.47
  116.4 2.6 convolution_bitcast_fusion
  119.1 0.9 copy-done.7
  120.0 0.6 collective-permute-start
  120.6 4.2 %collective-permute-start.1 = (bf16[256,512]{1,0:T(8,128)(2,1)S(1)}, bf16[256,512]{1,0:T(8,128)(2,1)}, u32[]{:S(2)}, u32[]{:S(2)}) collective-permute-start(bf16[256,512]{1,0:T(8,128)(2,1)S(1)} %copy-done.7), channel_id=1, source_target_pairs={{0,14},{2,0},{4,2},{6,4},{8,6},{10,8},{12,10},{14,12},{1,15},{3,1}... | collective-permute-start | bytes 786440 | tf_op jit(solution)/shard_map/ppermute | solution.py:83
  124.7 10.2 %collective-permute-done = bf16[256,512]{1,0:T(8,128)(2,1)} collective-permute-done((bf16[256,512]{1,0:T(8,128)(2,1)S(1)}, bf16[256,512]{1,0:T(8,128)(2,1)}, u32[]{:S(2)}, u32[]{:S(2)}) %collective-permute-start) | collective-permute-done | bytes 262176 | tf_op jit(solution)/shard_map/ppermute | solution.py:78
  135.0 2.6 collective-permute-start.2
  137.6 1.9 collective-permute-done.1
  139.5 0.7 collective-permute-start.3
  140.2 0.1 broadcast_in_dim.22
  140.6 8.5 %collective-permute-done.2 = bf16[256,512]{1,0:T(8,128)(2,1)} collective-permute-done((bf16[256,512]{1,0:T(8,128)(2,1)}, bf16[256,512]{1,0:T(8,128)(2,1)}, u32[]{:S(2)}, u32[]{:S(2)}) %collective-permute-start.2) | collective-permute-done | bytes 262176 | tf_op jit(solution)/shard_map/ppermute | solution.py:78
  149.1 2.5 collective-permute-start.4
  151.6 1.0 constant_dynamic-update-slice_fusion.6
  152.6 1.0 constant_dynamic-update-slice_fusion.5
  153.6 2.3 collective-permute-start.5
  155.9 1.0 constant_dynamic-update-slice_fusion.4
  156.9 12.7 %collective-permute-done.4 = bf16[256,512]{1,0:T(8,128)(2,1)S(1)} collective-permute-done((bf16[256,512]{1,0:T(8,128)(2,1)}, bf16[256,512]{1,0:T(8,128)(2,1)S(1)}, u32[]{:S(2)}, u32[]{:S(2)}) %collective-permute-start.4) | collective-permute-done | bytes 262176 | tf_op jit(solution)/shard_map/ppermute | solution.py:78
  169.5 2.4 collective-permute-start.6
  171.9 1.0 constant_dynamic-update-slice_fusion.3
  172.9 6.3 %collective-permute-done.6 = bf16[256,512]{1,0:T(8,128)(2,1)S(1)} collective-permute-done((bf16[256,512]{1,0:T(8,128)(2,1)S(1)}, bf16[256,512]{1,0:T(8,128)(2,1)S(1)}, u32[]{:S(2)}, u32[]{:S(2)}) %collective-permute-start.6) | collective-permute-done | bytes 262176 | tf_op jit(solution)/shard_map/ppermute | solution.py:78
  179.3 0.2 fusion.2
  179.6 0.2 convolution_bitcast_fusion.3
  179.8 0.8 fusion.3
  180.6 1.7 copy.52
  182.3 1.9 convolution_bitcast_fusion.1
  184.2 1.8 fusion.29
  186.0 2.5 convolution_convert_fusion
  188.5 1.7 rev.3
  190.3 0.8 while.29
  190.3 0.1 add_select_fusion.5
  190.4 0.1 add_select_fusion.5
  190.5 0.1 add_select_fusion.5
  190.6 0.1 add_select_fusion.5
  190.7 0.1 add_select_fusion.5
  190.9 0.1 add_select_fusion.5
  191.0 0.1 add_select_fusion.5
  191.1 0.1 copy.48
  191.2 1.2 fusion.4
  192.4 0.8 copy.53
  193.2 0.2 fusion.5
  193.4 0.8 copy.54
  194.2 83.4 %reduce-scatter.2.cloned.1.call-done = f32[256,512]{0,1:T(8,128)} async-done(((f32[2048,512]{0,1:T(8,128)}), f32[256,512]{0,1:T(8,128)}) %reduce-scatter.2.cloned.1.call-update) | async-done | bytes 524304 | tf_op jit(solution)/shard_map/reduce_scatter | solution.py:124
  277.6 2.0 copy.55
  279.7 19.4 %all-reduce.2.cloned.1.call-done = bf16[128,2048]{1,0:T(8,128)(2,1)} async-done(((bf16[128,2048]{1,0:T(8,128)(2,1)}), bf16[128,2048]{1,0:T(8,128)(2,1)}) %all-reduce.2.cloned.1.call-update) | async-done | bytes 524304 | tf_op jit(solution)/shard_map/psum | solution.py:91
  299.0 1.9 copy.128
  (47 shorter events, 0.6 us)
Async XLA Ops:
  7.2 105.5 %copy-start = (bf16[128,2048]{1,0:T(8,128)(2,1)S(1)}, bf16[128,2048]{1,0:T(8,128)(2,1)}, u32[]{:S(2)}) copy-start(bf16[128,2048]{1,0:T(8,128)(2,1)} %param.13) | copy-start | bytes 1572868
  7.2 55.6 %all-gather.8.cloned.1.call-start = ((), (), s32[]{:S(2)}) async-start(), calls=%async_computation.4 | async-start | bytes 2359296 | tf_op jit(solution)/shard_map/all_gather | solution.py:13
  8.3 2.7 copy-start.3
  10.2 102.5 %all-gather.6.cloned.1.call-start = ((), (), s32[]{:S(2)}) async-start(), calls=%async_computation.2 | async-start | bytes 2359296 | tf_op jit(solution)/shard_map/all_gather | solution.py:66
  10.9 177.6 %all-gather.10.cloned.1.call-start = ((), (), s32[]{:S(2)}) async-start(), calls=%async_computation.5 | async-start | bytes 2359296 | tf_op jit(solution)/shard_map/all_gather | solution.py:13
  12.2 50.5 %copy-start.10 = (bf16[4,128,128]{2,1,0:T(8,128)(2,1)}, bf16[4,128,128]{2,1,0:T(8,128)(2,1)S(1)}, u32[]{:S(2)}) copy-start(bf16[4,128,128]{2,1,0:T(8,128)(2,1)S(1)} %fusion.1) | copy-start | bytes 393220
  13.4 56.8 %copy-start.1 = (f32[4,128,128]{2,1,0:T(8,128)S(1)}, f32[4,128,128]{2,1,0:T(8,128)}, u32[]{:S(2)}) copy-start(f32[4,128,128]{2,1,0:T(8,128)} %fusion.10) | copy-start | bytes 786436
  62.7 7.5 %copy-start.5 = (bf16[128,512]{1,0:T(8,128)(2,1)S(1)}, bf16[128,512]{1,0:T(8,128)(2,1)}, u32[]{:S(2)}) copy-start(bf16[128,512]{1,0:T(8,128)(2,1)} %param.9) | copy-start | bytes 393220
  115.3 3.7 %copy-start.6 = (bf16[1,128,4,128]{1,3,2,0:T(8,128)(2,1)}, bf16[1,128,4,128]{1,3,2,0:T(8,128)(2,1)S(1)}, u32[]{:S(2)}) copy-start(bf16[1,128,4,128]{1,3,2,0:T(8,128)(2,1)S(1)} %get-tuple-element.222) | copy-start | bytes 393220
  116.4 161.3 %reduce-scatter.2.cloned.1.call-start = ((), (), s32[]{:S(2)}) async-start(), calls=%async_computation.3 | async-start | bytes 4718592 | tf_op jit(solution)/shard_map/reduce_scatter | solution.py:124
  119.1 1.0 copy-start.7
  119.1 179.9 %all-reduce.2.cloned.1.call-start = ((), (), s32[]{:S(2)}) async-start(), calls=%async_computation.1 | async-start | bytes 1048576 | tf_op jit(solution)/shard_map/psum | solution.py:91
  120.0 15.0 %collective-permute-start = (bf16[256,512]{1,0:T(8,128)(2,1)S(1)}, bf16[256,512]{1,0:T(8,128)(2,1)}, u32[]{:S(2)}, u32[]{:S(2)}) collective-permute-start(bf16[256,512]{1,0:T(8,128)(2,1)S(1)} %copy-done.7), channel_id=1, source_target_pairs={{0,2},{2,4},{4,6},{6,8},{8,10},{10,12},{12,14},{14,0},{1,3},{3,5},... | collective-permute-start | bytes 786440 | tf_op jit(solution)/shard_map/ppermute | solution.py:78
  120.6 18.9 %collective-permute-start.1 = (bf16[256,512]{1,0:T(8,128)(2,1)S(1)}, bf16[256,512]{1,0:T(8,128)(2,1)}, u32[]{:S(2)}, u32[]{:S(2)}) collective-permute-start(bf16[256,512]{1,0:T(8,128)(2,1)S(1)} %copy-done.7), channel_id=1, source_target_pairs={{0,14},{2,0},{4,2},{6,4},{8,6},{10,8},{12,10},{14,12},{1,15},{3,1}... | collective-permute-start | bytes 786440 | tf_op jit(solution)/shard_map/ppermute | solution.py:83
  135.0 14.2 %collective-permute-start.2 = (bf16[256,512]{1,0:T(8,128)(2,1)}, bf16[256,512]{1,0:T(8,128)(2,1)}, u32[]{:S(2)}, u32[]{:S(2)}) collective-permute-start(bf16[256,512]{1,0:T(8,128)(2,1)} %collective-permute-done), channel_id=1, source_target_pairs={{0,2},{2,4},{4,6},{6,8},{8,10},{10,12},{12,14},{14,0},{1,3},{3,5},... | collective-permute-start | bytes 786440 | tf_op jit(solution)/shard_map/ppermute | solution.py:78
  139.5 14.1 %collective-permute-start.3 = (bf16[256,512]{1,0:T(8,128)(2,1)}, bf16[256,512]{1,0:T(8,128)(2,1)}, u32[]{:S(2)}, u32[]{:S(2)}) collective-permute-start(bf16[256,512]{1,0:T(8,128)(2,1)} %collective-permute-done.1), channel_id=1, source_target_pairs={{0,14},{2,0},{4,2},{6,4},{8,6},{10,8},{12,10},{14,12},{1,15},{3,1}... | collective-permute-start | bytes 786440 | tf_op jit(solution)/shard_map/ppermute | solution.py:83
  140.4 38.9 %copy-start.2 = (bf16[128,512]{1,0:T(8,128)(2,1)S(1)}, bf16[128,512]{1,0:T(8,128)(2,1)}, u32[]{:S(2)}) copy-start(bf16[128,512]{1,0:T(8,128)(2,1)} %param.11) | copy-start | bytes 393220
  140.6 39.0 %copy-start.4 = (bf16[128,512]{0,1:T(8,128)(2,1)S(1)}, bf16[128,512]{0,1:T(8,128)(2,1)}, u32[]{:S(2)}) copy-start(bf16[128,512]{0,1:T(8,128)(2,1)} %copy-done.3) | copy-start | bytes 393220
  149.1 20.4 %collective-permute-start.4 = (bf16[256,512]{1,0:T(8,128)(2,1)}, bf16[256,512]{1,0:T(8,128)(2,1)S(1)}, u32[]{:S(2)}, u32[]{:S(2)}) collective-permute-start(bf16[256,512]{1,0:T(8,128)(2,1)} %collective-permute-done.2), channel_id=1, source_target_pairs={{0,2},{2,4},{4,6},{6,8},{8,10},{10,12},{12,14},{14,0},{1,3},{3,5},... | collective-permute-start | bytes 786440 | tf_op jit(solution)/shard_map/ppermute | solution.py:78
  153.6 19.3 %collective-permute-start.5 = (bf16[256,512]{1,0:T(8,128)(2,1)}, bf16[256,512]{1,0:T(8,128)(2,1)S(1)}, u32[]{:S(2)}, u32[]{:S(2)}) collective-permute-start(bf16[256,512]{1,0:T(8,128)(2,1)} %collective-permute-done.3), channel_id=1, source_target_pairs={{0,14},{2,0},{4,2},{6,4},{8,6},{10,8},{12,10},{14,12},{1,15},{3,1}... | collective-permute-start | bytes 786440 | tf_op jit(solution)/shard_map/ppermute | solution.py:83
  169.5 9.7 %collective-permute-start.6 = (bf16[256,512]{1,0:T(8,128)(2,1)S(1)}, bf16[256,512]{1,0:T(8,128)(2,1)S(1)}, u32[]{:S(2)}, u32[]{:S(2)}) collective-permute-start(bf16[256,512]{1,0:T(8,128)(2,1)S(1)} %collective-permute-done.4), channel_id=1, source_target_pairs={{0,2},{2,4},{4,6},{6,8},{8,10},{10,12},{12,14},{14,0},{1,3},{3,5},... | collective-permute-start | bytes 786440 | tf_op jit(solution)/shard_map/ppermute | solution.py:78
  179.6 1.1 copy-start.11
  190.3 2.9 copy-start.9
  191.1 2.2 copy-start.8
Sparse Core Ops, SparseCore 0:
  10.7 51.9 all-gather.7
  64.9 47.7 all-gather.5
  116.5 67.7 all-gather.9
  187.8 89.7 reduce-scatter.1
  280.5 18.4 all-reduce.1
